TPU v7x, 32 devices: a whole 2x2x4 slice. The times are simulated.
32 devices in a mesh: rad: 8 (over z, y), ell: 4 (over x, core).
Axes of the slice: x: 2, y: 2, z: 4, core: 2. Of those that a mesh axis runs over, the one named last changes fastest.
Arguments:
- field: bfloat16 [512, 128, 512], P('rad', 'ell'), may hold values from -6 to 6
- projection: bfloat16 [512, 128, 256], P('rad', 'ell'), may hold values from -0.375 to 0.375
- ell_ids: int32 [128], P('ell'), may hold values from 0 to 255, as said below
Outputs:
- share: float32 [128, 256], P('ell', 'rad')
- crest: float32 [128, 256], P('ell', 'rad')
Inputs may be any that keep to these rules, and one draw needn't show every extreme that they name: `ell_ids`: distinct and ascending.
All inputs are finite; a program needn't handle non-finite values.
Results may differ from a plain program's by a relative error of at most 0.0003.
Values may be sent and summed in bfloat16 or wider, within the bound.
A program may use at most 64 MiB of HBM per device.

v0:
```python
import jax
import jax.numpy as jnp
from jax import lax
from jax.sharding import PartitionSpec as P


def per_device(field, projection, ell_ids):
    exchanged = lax.all_to_all(field, "rad", split_axis=2, concat_axis=0, tiled=True)
    slot_share = exchanged.shape[2]
    coef = jnp.einsum(
        "rem,ren->emn",
        exchanged,
        lax.all_gather(projection, "rad", axis=0, tiled=True),
        preferred_element_type=jnp.float32,
    )
    slots = lax.axis_index("rad") * slot_share + jnp.arange(slot_share, dtype=jnp.int32)
    valid = (slots[None, :] < 2 * ell_ids[:, None] + 1).astype(jnp.float32)
    energy_part = jnp.sum(valid[:, :, None] * coef * coef, axis=1)
    peak_part = jnp.max(valid[:, :, None] * jnp.abs(coef), axis=1)
    energy_all, peak_all = (
        lax.all_to_all(energy_part[None], "rad", split_axis=2, concat_axis=0, tiled=True),
        lax.all_to_all(peak_part[None], "rad", split_axis=2, concat_axis=0, tiled=True),
    )
    energy = jnp.sum(energy_all, axis=0)
    peak = jnp.max(peak_all, axis=0)
    local_sum = jnp.sum(energy, axis=0)
    local_top = jnp.max(peak, axis=0)
    column = lax.psum(local_sum, "ell")
    top = lax.pmax(local_top, "ell")
    column = column + 1e-06
    top = top + 1e-06
    total_ells = ell_ids.shape[0] * lax.axis_size("ell")
    share = total_ells * energy / column[None, :]
    crest = peak / top[None, :]
    return (share, crest)


def solution(mesh):
    in_specs = (P("rad", "ell", None), P("rad", "ell", None), P("ell"))
    out_specs = (P("ell", "rad"), P("ell", "rad"))
    return jax.shard_map(
        per_device, mesh=mesh, in_specs=in_specs, out_specs=out_specs, check_vma=False
    )
```

profile of v0, /device:TPU:0, one launch (start us, length us, event | category | flops | bytes accessed | tf_op | source)
XLA Modules:
  0.0 218.3 jit_solution(14163633866488096663)
XLA Ops:
  7.2 2.9 %copy.19 = bf16[64,32,256]{2,0,1:T(8,128)(2,1)} copy(bf16[64,32,256]{2,1,0:T(8,128)(2,1)} %param.4) | data formatting | bytes 2097152 | tf_op args[1]
  10.2 7.8 %copy.17 = bf16[64,32,512]{0,1,2:T(8,128)(2,1)} copy(bf16[64,32,512]{2,1,0:T(8,128)(2,1)S(1)} %copy-done) | data formatting | bytes 4194304 | tf_op args[0]
  18.0 7.7 %reshape.45 = bf16[8,2,65536]{2,1,0:T(2,128)(2,1)} reshape(bf16[512,32,64]{2,1,0:T(8,128)(2,1)} %bitcast.22) | data formatting | bytes 4194304
  25.7 7.5 %all-to-all-start = ((bf16[8,2,65536]{2,1,0:T(2,128)(2,1)}), bf16[8,2,65536]{2,1,0:T(2,128)(2,1)S(1)}, u32[]{:S(2)}, u32[]{:S(2)}) async-start(bf16[8,2,65536]{2,1,0:T(2,128)(2,1)} %reshape.45), calls=%async_computation | async-start | bytes 4194304 | tf_op jit(solution)/shard_map/all_to_all | solution.py:8
  33.2 87.4 %all-to-all-done = bf16[8,2,65536]{2,1,0:T(2,128)(2,1)S(1)} async-done(((bf16[8,2,65536]{2,1,0:T(2,128)(2,1)}), bf16[8,2,65536]{2,1,0:T(2,128)(2,1)S(1)}, u32[]{:S(2)}, u32[]{:S(2)}) %all-to-all-start) | async-done | bytes 2097184 | tf_op jit(solution)/shard_map/all_to_all | solution.py:8
  120.7 5.0 %reshape.46 = bf16[512,32,64]{2,1,0:T(8,128)(2,1)} reshape(bf16[8,2,65536]{2,1,0:T(2,128)(2,1)S(1)} %all-to-all-done) | data formatting | bytes 4194304
  125.7 6.8 %copy.25 = bf16[64,32,8,64]{0,2,3,1:T(8,128)(2,1)} copy(bf16[64,32,8,64]{0,1,3,2:T(8,128)(2,1)} %bitcast.23) | data formatting | bytes 4194304 | tf_op jit(solution)/shard_map/all_to_all | solution.py:8
  132.5 5.4 %all_to_all.34 = bf16[512,32,64]{0,2,1:T(8,128)(2,1)S(1)} reshape(bf16[8,64,32,64]{1,0,3,2:T(8,128)(2,1)} %bitcast.24) | data formatting | bytes 4194304 | tf_op jit(solution)/shard_map/all_to_all | solution.py:8
  137.9 35.0 %all-gather.2.cloned.1.call-done = bf16[512,32,256]{2,0,1:T(8,128)(2,1)} async-done(((bf16[64,32,256]{2,0,1:T(8,128)(2,1)}), bf16[512,32,256]{2,0,1:T(8,128)(2,1)}) %all-gather.2.cloned.1.call-update) | async-done | bytes 8388624 | tf_op jit(solution)/shard_map/all_gather | solution.py:13
  172.9 4.9 %multiply_reduce_fusion = (f32[32,256]{1,0:T(8,128)S(1)}, f32[32,256]{1,0:T(8,128)S(1)}) fusion(f32[32,64]{1,0:T(8,128)S(1)} %compare_convert_fusion, bf16[512,32,64]{0,2,1:T(8,128)(2,1)S(1)} %all_to_all.34, bf16[512,32,256]{2,0,1:T(8,128)(2,1)} %all-gather.2.cloned.1.call-done), kind=kOutput, calls=%fused_computation.3 | convolution fusion | flops 540000256 | bytes 10559488 | tf_op jit(solution)/shard_map/rem,ren->emn/dot_general | solution.py:10
  177.8 0.1 copy.21
  177.9 0.5 broadcast.33
  178.4 1.0 reduce.18
  179.4 0.7 reshape.49
  180.1 3.3 %all-to-all-start.2 = ((f32[8,1,1024]{2,1,0:T(1,128)}), f32[8,1,1024]{2,1,0:T(1,128)S(1)}, u32[]{:S(2)}, u32[]{:S(2)}) async-start(f32[8,1,1024]{2,1,0:T(1,128)} %reshape.49), calls=%async_computation.2 | async-start | bytes 65536 | tf_op jit(solution)/shard_map/all_to_all | solution.py:22
  183.5 0.1 copy.20
  183.6 1.0 reduce.16
  184.6 0.7 reshape.47
  185.3 4.8 %all-to-all-done.2 = f32[8,1,1024]{2,1,0:T(1,128)S(1)} async-done(((f32[8,1,1024]{2,1,0:T(1,128)}), f32[8,1,1024]{2,1,0:T(1,128)S(1)}, u32[]{:S(2)}, u32[]{:S(2)}) %all-to-all-start.2) | async-done | bytes 32800 | tf_op jit(solution)/shard_map/all_to_all | solution.py:22
  190.1 3.3 %all-to-all-start.1 = ((f32[8,1,1024]{2,1,0:T(1,128)}), f32[8,1,1024]{2,1,0:T(1,128)S(1)}, u32[]{:S(2)}, u32[]{:S(2)}) async-start(f32[8,1,1024]{2,1,0:T(1,128)} %reshape.47), calls=%async_computation.1 | async-start | bytes 65536 | tf_op jit(solution)/shard_map/all_to_all | solution.py:21
  193.4 0.7 reduce.19
  194.2 0.2 reshape.50
  194.4 1.0 bitcast_reduce_fusion
  195.4 0.1 reduce_max.37
  195.6 6.0 %pmax.7 = f32[32]{0:T(128)S(1)} all-reduce(f32[32]{0:T(128)S(1)} %reduce_max.38), channel_id=1, replica_groups=mesh['rad'=8,'ell'=4] {'ell'}, use_global_device_ids=true, to_apply=%region_9.10 | all-reduce | flops 32 | bytes 256 | tf_op jit(solution)/shard_map/pmax | solution.py:29
  201.6 0.7 copy.23
  202.3 0.7 reduce.17
  203.0 0.2 reshape.48
  203.2 1.0 bitcast_reduce_fusion.1
  204.3 0.1 reduce_sum.37
  204.4 6.3 %psum.7 = f32[32]{0:T(128)S(1)} all-reduce(f32[32]{0:T(128)S(1)} %reduce_sum.38), channel_id=1, replica_groups=mesh['rad'=8,'ell'=4] {'ell'}, use_global_device_ids=true, to_apply=%region_4.0 | all-reduce | flops 32 | bytes 256 | tf_op jit(solution)/shard_map/psum | solution.py:28
  210.8 0.7 copy.22
  (18 shorter events, 0.4 us)
Async XLA Ops:
  7.2 3.0 %copy-start = (bf16[64,32,512]{2,1,0:T(8,128)(2,1)S(1)}, bf16[64,32,512]{2,1,0:T(8,128)(2,1)}, u32[]{:S(2)}) copy-start(bf16[64,32,512]{2,1,0:T(8,128)(2,1)} %param.3) | copy-start | bytes 6291460
  7.2 165.7 %all-gather.2.cloned.1.call-start = ((), (), s32[]{:S(2)}) async-start(), calls=%async_computation.3 | async-start | bytes 9437184 | tf_op jit(solution)/shard_map/all_gather | solution.py:13
  25.7 7.5 %copy-start.1 = (s32[32]{0:T(128)S(1)}, s32[32]{0:T(128)}, u32[]{:S(2)}) copy-start(s32[32]{0:T(128)} %param.5) | copy-start | bytes 388
  25.7 95.0 %all-to-all-start = ((bf16[8,2,65536]{2,1,0:T(2,128)(2,1)}), bf16[8,2,65536]{2,1,0:T(2,128)(2,1)S(1)}, u32[]{:S(2)}, u32[]{:S(2)}) async-start(bf16[8,2,65536]{2,1,0:T(2,128)(2,1)} %reshape.45), calls=%async_computation | async-start | bytes 4194304 | tf_op jit(solution)/shard_map/all_to_all | solution.py:8
  180.1 10.0 %all-to-all-start.2 = ((f32[8,1,1024]{2,1,0:T(1,128)}), f32[8,1,1024]{2,1,0:T(1,128)S(1)}, u32[]{:S(2)}, u32[]{:S(2)}) async-start(f32[8,1,1024]{2,1,0:T(1,128)} %reshape.49), calls=%async_computation.2 | async-start | bytes 65536 | tf_op jit(solution)/shard_map/all_to_all | solution.py:22
  190.1 12.2 %all-to-all-start.1 = ((f32[8,1,1024]{2,1,0:T(1,128)}), f32[8,1,1024]{2,1,0:T(1,128)S(1)}, u32[]{:S(2)}, u32[]{:S(2)}) async-start(f32[8,1,1024]{2,1,0:T(1,128)} %reshape.47), calls=%async_computation.1 | async-start | bytes 65536 | tf_op jit(solution)/shard_map/all_to_all | solution.py:21
Sparse Core Ops, SparseCore 0:
  10.3 162.5 all-gather.1
where the time goes:
time: 219 us; the launch traced here: 218 us
  waiting for transfers between devices  127 us (58%)
  local copies, waits for them, and re-layouts  39.8 us (18%)
  starting transfers between devices  14.2 us (6%)
  between operations  14.2 us (6%)
  blocking collectives  12.3 us (6%)
  other arithmetic  5.77 us (3%)
  matrix products  4.92 us (2%)
    all_to_all x1, waiting for transfers between devices, per_device(): lax.all_to_all(field, 'rad', split_axis=2, concat_axis=0, tiled=True)  87.4 us
    all_gather x1, waiting for transfers between devices, per_device(): lax.all_gather(projection, 'rad', axis=0, tiled=True)  35 us
    unnamed x15, local copies, waits for them, and re-layouts  27.2 us
    all_to_all x2, local copies, waits for them, and re-layouts, per_device(): lax.all_to_all(field, 'rad', split_axis=2, concat_axis=0, tiled=True)  12.2 us
    all_to_all x1, starting transfers between devices, per_device(): lax.all_to_all(field, 'rad', split_axis=2, concat_axis=0, tiled=True)  7.47 us
    psum x1, blocking collectives, per_device(): column = lax.psum(local_sum, 'ell')  6.3 us
    pmax x1, blocking collectives, per_device(): top = lax.pmax(local_top, 'ell')  5.96 us
    dot_general x1, matrix products, per_device(): jnp.einsum('rem,ren->emn', exchanged, lax.all_gather(projection, 'rad', a...  4.92 us
  transfers between devices with their start and end apart: 4, of which 3 were waited for; matrix products, arithmetic and copies ran while one was open for 15% of the time, Pallas kernels for 0%

commit v1 on v0

--- a/solution.py
+++ b/solution.py
@@ -4,8 +4,14 @@
 from jax.sharding import PartitionSpec as P
 
 
+def exchange_blocks(x, axis, split, join):
+    pieces = jnp.split(x, lax.axis_size(axis), axis=split)
+    received = lax.all_to_all(jnp.stack(pieces), axis, 0, 0)
+    return jnp.concatenate(received, axis=join)
+
+
 def per_device(field, projection, ell_ids):
-    exchanged = lax.all_to_all(field, "rad", split_axis=2, concat_axis=0, tiled=True)
+    exchanged = exchange_blocks(field, "rad", 2, 0)
     slot_share = exchanged.shape[2]
     coef = jnp.einsum(
         "rem,ren->emn",

time: 219 us -> 226 us (1.032)
  waiting for transfers between devices: 127 us -> 141 us
  local copies, waits for them, and re-layouts: 39.8 us -> 28.6 us
  matrix products: 4.92 us -> 9.64 us
    all_to_all x1, waiting for transfers between devices: 87.4 us -> 100 us  [exchange_blocks(): received = lax.all_to_all(jnp.stack(pieces), axis, 0, 0)]
    all_to_all x2 -> x0, local copies, waits for them, and re-layouts: 12.2 us -> none  [per_device(): lax.all_to_all(field, 'rad', split_axis=2, concat_axis=0, tiled=True)]
    dot_general x1, matrix products: 4.92 us -> 9.64 us  [per_device(): jnp.einsum('rem,ren->emn', exchanged, lax.all_gather(projection, 'rad', a...]
    unnamed x15 -> x21, local copies, waits for them, and re-layouts: 27.2 us -> 27.2 us
  transfers between devices with their start and end apart: 4 -> 4, of which waited for: 3 -> 3; matrix products, arithmetic and copies ran while one was open for 15% -> 12% of each run, Pallas kernels for 0% -> 0%
where the time goes in v1:
time: 226 us; the launch traced here: 225 us
  waiting for transfers between devices  141 us (62%)
  local copies, waits for them, and re-layouts  28.6 us (13%)
  between operations  14.2 us (6%)
  starting transfers between devices  14 us (6%)
  blocking collectives  12.2 us (5%)
  matrix products  9.64 us (4%)
  other arithmetic  5.77 us (3%)
    all_to_all x1, waiting for transfers between devices, exchange_blocks(): received = lax.all_to_all(jnp.stack(pieces), axis, 0, 0)  100 us
    all_gather x1, waiting for transfers between devices, per_device(): lax.all_gather(projection, 'rad', axis=0, tiled=True)  35.8 us
    unnamed x21, local copies, waits for them, and re-layouts  27.2 us
    dot_general x1, matrix products, per_device(): jnp.einsum('rem,ren->emn', exchanged, lax.all_gather(projection, 'rad', a...  9.64 us
    all_to_all x1, starting transfers between devices, exchange_blocks(): received = lax.all_to_all(jnp.stack(pieces), axis, 0, 0)  7.29 us
    psum x1, blocking collectives, per_device(): column = lax.psum(local_sum, 'ell')  6.21 us
    pmax x1, blocking collectives, per_device(): top = lax.pmax(local_top, 'ell')  5.96 us
    all_to_all x1, waiting for transfers between devices, per_device(): lax.all_to_all(peak_part[None], 'rad', split_axis=2, concat_axis=0, tiled...  4.82 us
  transfers between devices with their start and end apart: 4, of which 3 were waited for; matrix products, arithmetic and copies ran while one was open for 12% of the time, Pallas kernels for 0%

profile of v1, /device:TPU:0, one launch (start us, length us, event | category | flops | bytes accessed | tf_op | source)
XLA Modules:
  0.0 225.3 jit_solution(3719334855987009365)
XLA Ops:
  7.2 2.9 %copy.16 = bf16[64,32,256]{2,0,1:T(8,128)(2,1)} copy(bf16[64,32,256]{2,1,0:T(8,128)(2,1)} %param.4) | data formatting | bytes 2097152 | tf_op args[1]
  10.2 1.9 bitcast_dynamic-update-slice_fusion.7
  12.1 1.1 bitcast_dynamic-update-slice_fusion.6
  13.2 0.9 bitcast_dynamic-update-slice_fusion.5
  14.1 1.0 bitcast_dynamic-update-slice_fusion.4
  15.1 0.9 bitcast_dynamic-update-slice_fusion.3
  16.0 1.0 bitcast_dynamic-update-slice_fusion.2
  17.0 0.9 bitcast_dynamic-update-slice_fusion.1
  17.9 1.0 bitcast_dynamic-update-slice_fusion
  19.0 7.7 %reshape.49 = bf16[8,2,65536]{2,1,0:T(2,128)(2,1)} reshape(bf16[8,64,32,64]{3,2,1,0:T(8,128)(2,1)} %bitcast_dynamic-update-slice_fusion) | data formatting | bytes 4194304
  26.7 7.3 %all-to-all-start = ((bf16[8,2,65536]{2,1,0:T(2,128)(2,1)}), bf16[8,2,65536]{2,1,0:T(2,128)(2,1)S(1)}, u32[]{:S(2)}, u32[]{:S(2)}) async-start(bf16[8,2,65536]{2,1,0:T(2,128)(2,1)} %reshape.49), calls=%async_computation | async-start | bytes 4194304 | tf_op jit(solution)/shard_map/all_to_all | solution.py:9
  34.1 100.2 %all-to-all-done = bf16[8,2,65536]{2,1,0:T(2,128)(2,1)S(1)} async-done(((bf16[8,2,65536]{2,1,0:T(2,128)(2,1)}), bf16[8,2,65536]{2,1,0:T(2,128)(2,1)S(1)}, u32[]{:S(2)}, u32[]{:S(2)}) %all-to-all-start) | async-done | bytes 2097184 | tf_op jit(solution)/shard_map/all_to_all | solution.py:9
  134.3 5.0 %reshape.50 = bf16[8,64,32,64]{3,2,1,0:T(8,128)(2,1)} reshape(bf16[8,2,65536]{2,1,0:T(2,128)(2,1)S(1)} %all-to-all-done) | data formatting | bytes 4194304
  139.4 35.8 %all-gather.2.cloned.1.call-done = bf16[512,32,256]{2,0,1:T(8,128)(2,1)} async-done(((bf16[64,32,256]{2,0,1:T(8,128)(2,1)}), bf16[512,32,256]{2,0,1:T(8,128)(2,1)}) %all-gather.2.cloned.1.call-update) | async-done | bytes 8388624 | tf_op jit(solution)/shard_map/all_gather | solution.py:19
  175.2 9.6 %multiply_reduce_fusion = (f32[32,256]{1,0:T(8,128)S(1)}, f32[32,256]{1,0:T(8,128)S(1)}) fusion(f32[32,64]{1,0:T(8,128)S(1)} %compare_convert_fusion, bf16[512,32,256]{2,0,1:T(8,128)(2,1)} %all-gather.2.cloned.1.call-done, bf16[512,32,64]{2,1,0:T(8,128)(2,1)} %bitcast.28), kind=kOutput, calls=%fused_computation.4 | convolution fusion | flops 540000256 | bytes 10559488 | tf_op jit(solution)/shard_map/rem,ren->emn/dot_general | solution.py:16
  185.0 0.5 broadcast.33
  185.5 1.0 reduce.18
  186.5 0.7 reshape.53
  187.2 3.3 %all-to-all-start.2 = ((f32[8,1,1024]{2,1,0:T(1,128)}), f32[8,1,1024]{2,1,0:T(1,128)S(1)}, u32[]{:S(2)}, u32[]{:S(2)}) async-start(f32[8,1,1024]{2,1,0:T(1,128)} %reshape.53), calls=%async_computation.2 | async-start | bytes 65536 | tf_op jit(solution)/shard_map/all_to_all | solution.py:28
  190.6 1.0 reduce.16
  191.6 0.7 reshape.51
  192.3 4.8 %all-to-all-done.2 = f32[8,1,1024]{2,1,0:T(1,128)S(1)} async-done(((f32[8,1,1024]{2,1,0:T(1,128)}), f32[8,1,1024]{2,1,0:T(1,128)S(1)}, u32[]{:S(2)}, u32[]{:S(2)}) %all-to-all-start.2) | async-done | bytes 32800 | tf_op jit(solution)/shard_map/all_to_all | solution.py:28
  197.1 3.3 %all-to-all-start.1 = ((f32[8,1,1024]{2,1,0:T(1,128)}), f32[8,1,1024]{2,1,0:T(1,128)S(1)}, u32[]{:S(2)}, u32[]{:S(2)}) async-start(f32[8,1,1024]{2,1,0:T(1,128)} %reshape.51), calls=%async_computation.1 | async-start | bytes 65536 | tf_op jit(solution)/shard_map/all_to_all | solution.py:27
  200.5 0.7 reduce.19
  201.2 0.2 reshape.54
  201.4 1.0 bitcast_reduce_fusion
  202.6 6.0 %pmax.7 = f32[32]{0:T(128)S(1)} all-reduce(f32[32]{0:T(128)S(1)} %reduce_max.38), channel_id=1, replica_groups=mesh['rad'=8,'ell'=4] {'ell'}, use_global_device_ids=true, to_apply=%region_9.10 | all-reduce | flops 32 | bytes 256 | tf_op jit(solution)/shard_map/pmax | solution.py:35
  208.6 0.7 copy.20
  209.3 0.7 reduce.17
  210.3 1.0 bitcast_reduce_fusion.1
  211.4 6.2 %psum.7 = f32[32]{0:T(128)S(1)} all-reduce(f32[32]{0:T(128)S(1)} %reduce_sum.38), channel_id=1, replica_groups=mesh['rad'=8,'ell'=4] {'ell'}, use_global_device_ids=true, to_apply=%region_4.0 | all-reduce | flops 32 | bytes 256 | tf_op jit(solution)/shard_map/psum | solution.py:34
  217.7 0.7 copy.19
  (23 shorter events, 1.0 us)
Async XLA Ops:
  7.2 4.9 %copy-start = (bf16[64,32,512]{2,1,0:T(8,128)(2,1)S(1)}, bf16[64,32,512]{2,1,0:T(8,128)(2,1)}, u32[]{:S(2)}) copy-start(bf16[64,32,512]{2,1,0:T(8,128)(2,1)} %param.3) | copy-start | bytes 6291460
  7.2 168.0 %all-gather.2.cloned.1.call-start = ((), (), s32[]{:S(2)}) async-start(), calls=%async_computation.3 | async-start | bytes 9437184 | tf_op jit(solution)/shard_map/all_gather | solution.py:19
  18.9 15.1 %copy-start.1 = (s32[32]{0:T(128)S(1)}, s32[32]{0:T(128)}, u32[]{:S(2)}) copy-start(s32[32]{0:T(128)} %param.5) | copy-start | bytes 388
  26.7 107.6 %all-to-all-start = ((bf16[8,2,65536]{2,1,0:T(2,128)(2,1)}), bf16[8,2,65536]{2,1,0:T(2,128)(2,1)S(1)}, u32[]{:S(2)}, u32[]{:S(2)}) async-start(bf16[8,2,65536]{2,1,0:T(2,128)(2,1)} %reshape.49), calls=%async_computation | async-start | bytes 4194304 | tf_op jit(solution)/shard_map/all_to_all | solution.py:9
  187.2 10.0 %all-to-all-start.2 = ((f32[8,1,1024]{2,1,0:T(1,128)}), f32[8,1,1024]{2,1,0:T(1,128)S(1)}, u32[]{:S(2)}, u32[]{:S(2)}) async-start(f32[8,1,1024]{2,1,0:T(1,128)} %reshape.53), calls=%async_computation.2 | async-start | bytes 65536 | tf_op jit(solution)/shard_map/all_to_all | solution.py:28
  197.1 12.2 %all-to-all-start.1 = ((f32[8,1,1024]{2,1,0:T(1,128)}), f32[8,1,1024]{2,1,0:T(1,128)S(1)}, u32[]{:S(2)}, u32[]{:S(2)}) async-start(f32[8,1,1024]{2,1,0:T(1,128)} %reshape.51), calls=%async_computation.1 | async-start | bytes 65536 | tf_op jit(solution)/shard_map/all_to_all | solution.py:27
Sparse Core Ops, SparseCore 0:
  10.3 164.8 all-gather.1
